TPU v7x, 32 devices: a whole 2x2x4 slice. The times are simulated.
32 devices in a mesh: depth: 4 (over z), lat: 8 (over y, x, core).
Axes of the slice: x: 2, y: 2, z: 4, core: 2. Of those that a mesh axis runs over, the one named last changes fastest.
Arguments:
- volume_init: float32 [16, 64, 16, 128], P('depth', 'lat'), may hold values from 0.2 to 10
- measured: float32 [64, 16, 128], P('lat'), may hold values from 0.25 to 4
- psf: bfloat16 [16, 13, 128, 128], P('depth'), may hold values from 0 to 0.0043269231
- offsets: int32 [16, 13], replicated, may hold values from 0 to 24, as said below
- counts: int32 [16], replicated, may hold values from 1 to 13, 130 in all
Outputs:
- volume: float32 [16, 64, 16, 128], P('depth', 'lat')
Inputs may be any that keep to these rules, and one draw needn't show every extreme that they name: `offsets`: entry v names the block offset (v // 5 - 2, v % 5 - 2) in patch rows and patches; the entries of one depth are distinct, and entry 0 of every depth is the central offset 2 * 5 + 2.
All inputs are finite; a program needn't handle non-finite values.
Results may differ from a plain program's by a relative error of at most 0.00076.
Values may be sent and summed in bfloat16 or wider, within the bound.
A program may use at most 64 MiB of HBM per device.

v0:
```python
import jax
import jax.numpy as jnp
from jax import lax
from jax.sharding import PartitionSpec as P

RY = 2
RX = 2
ITERS = 2


def with_halo(cells, sides, width):
    for axis, dim in sides:
        count = lax.axis_size(axis)
        ends = count - 1
        head = lax.slice_in_dim(cells, 0, width, axis=dim)
        tail = lax.slice_in_dim(cells, cells.shape[dim] - width, cells.shape[dim], axis=dim)
        cells = jnp.concatenate(
            [
                lax.ppermute(tail, axis, [(i, (i + 1) % count) for i in range(ends)]),
                cells,
                lax.ppermute(head, axis, [((i + 1) % count, i) for i in range(ends)]),
            ],
            axis=dim,
        )
    return cells


def split_offsets(offsets):
    span_x = 2 * RX + 1
    return (offsets // span_x - RY, offsets % span_x - RX)


def project(plane, blocks, rows_by, cols_by, transpose):
    plane_rows = plane.shape[0]
    plane_cols = plane.shape[1]
    tile_rows = plane_rows - 2 * RY
    tile_cols = plane_cols - 2 * RX
    pixels = plane.shape[2]
    flat_plane = plane.reshape(plane_rows * plane_cols, pixels)
    span_x = 2 * RX + 1
    span_all = (2 * RY + 1) * span_x
    codes = (rows_by + RY) * span_x + (cols_by + RX)
    one_hot = (codes[:, None] == jnp.arange(span_all, dtype=jnp.int32)[None, :]).astype(jnp.float32)
    block_values = blocks.astype(jnp.float32)
    if transpose:
        dense = jnp.einsum("ko,kji->ioj", one_hot, block_values, precision=lax.Precision.HIGHEST)
    else:
        dense = jnp.einsum("ko,kji->joi", one_hot, block_values, precision=lax.Precision.HIGHEST)
    dense = dense.astype(jnp.bfloat16).reshape(pixels, span_all * pixels)
    products = jnp.dot(flat_plane, dense, preferred_element_type=jnp.float32).reshape(
        plane_rows, plane_cols, span_all, pixels
    )
    total = jnp.zeros((tile_rows, tile_cols, pixels), jnp.float32)
    for code in range(span_all):
        row_start = code // span_x
        col_start = code % span_x
        total = (
            total
            + products[row_start : row_start + tile_rows, col_start : col_start + tile_cols, code]
        )
    return total


def shards(volume_init, measured, psf, offsets, counts):
    depth_here = volume_init.shape[0]
    tile_rows = volume_init.shape[1]
    tile_cols = volume_init.shape[2]
    pixels = volume_init.shape[3]
    slot_total = psf.shape[1]
    base_depth = lax.axis_index("depth") * depth_here
    local_offsets = lax.dynamic_slice_in_dim(offsets, base_depth, depth_here, 0)
    local_counts = lax.dynamic_slice_in_dim(counts, base_depth, depth_here, 0)
    slot_ids = jnp.arange(slot_total, dtype=jnp.int32)
    live = slot_ids[None, :] < local_counts[:, None]
    weights = jnp.where(live[:, :, None, None], psf, jnp.zeros_like(psf))
    shift_rows, shift_cols = split_offsets(local_offsets)
    all_rows = tile_rows * lax.axis_size("lat")
    row_ids = lax.axis_index("lat") * tile_rows + jnp.arange(tile_rows, dtype=jnp.int32)
    col_ids = jnp.arange(tile_cols, dtype=jnp.int32)
    coverages = []
    for plane_id in range(depth_here):
        source_rows = row_ids[None, :] - shift_rows[plane_id][:, None]
        source_cols = col_ids[None, :] - shift_cols[plane_id][:, None]
        inside_rows = (source_rows >= 0) & (source_rows < all_rows)
        inside_cols = (source_cols >= 0) & (source_cols < tile_cols)
        inside = (inside_rows[:, :, None] & inside_cols[:, None, :]).astype(jnp.float32)
        column_sums = jnp.sum(weights[plane_id].astype(jnp.float32), axis=2)
        coverages.append(
            jnp.einsum("kyx,kj->yxj", inside, column_sums, precision=lax.Precision.HIGHEST)
        )
    volume = volume_init
    for repeat in range(ITERS):
        extended = with_halo(volume.astype(jnp.bfloat16), (("lat", 1),), RY)
        padded = jnp.pad(extended, ((0, 0), (0, 0), (RX, RX), (0, 0)))
        partial_sensor = jnp.zeros((tile_rows, tile_cols, pixels), jnp.float32)
        for plane_id in range(depth_here):
            partial_sensor = partial_sensor + project(
                padded[plane_id],
                weights[plane_id],
                shift_rows[plane_id],
                shift_cols[plane_id],
                False,
            )
        sensor = lax.psum(partial_sensor, "depth")
        ratio = (measured / sensor).astype(jnp.bfloat16)
        ratio_ext = with_halo(ratio, (("lat", 0),), RY)
        ratio_pad = jnp.pad(ratio_ext, ((0, 0), (RX, RX), (0, 0)))
        updated = []
        for plane_id in range(depth_here):
            back = project(
                ratio_pad, weights[plane_id], -shift_rows[plane_id], -shift_cols[plane_id], True
            )
            updated.append(volume[plane_id] * back / coverages[plane_id])
        volume = jnp.stack(updated)
    return volume


def solution(mesh):
    return jax.shard_map(
        shards,
        mesh=mesh,
        in_specs=(
            P("depth", "lat", None, None),
            P("lat", None, None),
            P("depth", None, None, None),
            P(),
            P(),
        ),
        out_specs=P("depth", "lat", None, None),
        check_vma=False,
    )
```

profile of v0, /device:TPU:0, one launch (start us, length us, event | category | flops | bytes accessed | tf_op | source)
XLA Modules:
  0.0 166.0 jit_solution(4459511551675382461)
XLA Ops:
  7.5 3.0 %collective-permute-start = (bf16[4,2,16,128]{3,2,1,0:T(8,128)(2,1)S(1)}, bf16[4,2,16,128]{3,2,1,0:T(8,128)(2,1)}, u32[]{:S(2)}, u32[]{:S(2)}) collective-permute-start(bf16[4,2,16,128]{3,2,1,0:T(8,128)(2,1)S(1)} %get-tuple-element.19), channel_id=1, source_target_pairs={{0,1},{1,2},{2,3},{3,4},{4,5},{5,6},{6,7},{8,9},{9,10},{10,11},{11... | collective-permute-start | bytes 98312 | tf_op jit(solution)/shard_map/ppermute | solution.py:19
  13.9 2.5 %copy_select_fusion = bf16[4,13,128,128]{3,1,2,0:T(8,128)(2,1)S(1)} fusion(bf16[4,13,128,128]{3,2,1,0:T(8,128)(2,1)} %param.7, pred[4,13]{1,0:T(4,128)(4,1)S(1)} %iota_compare_fusion.12), kind=kLoop, calls=%fused_computation | loop fusion | flops 851968 | bytes 3407924 | tf_op jit(solution)/shard_map/jit(_where)/select_n | solution.py:75
  18.2 1.5 fusion.2
  19.7 1.5 fusion.1
  21.3 1.5 fusion
  22.8 1.5 fusion.4
  24.9 1.5 fusion.5
  27.1 1.5 fusion.6
  29.3 1.5 fusion.7
  35.2 2.1 %copy.866 = bf16[128,25,128]{0,2,1:T(8,128)(2,1)S(1)} copy(bf16[128,25,128]{2,1,0:T(8,128)(2,1)} %fusion.2) | data formatting | bytes 1638400 | tf_op jit(solution)/shard_map/convert_element_type | solution.py:49
  37.4 2.1 %copy.840 = bf16[128,25,128]{0,2,1:T(8,128)(2,1)S(1)} copy(bf16[128,25,128]{2,1,0:T(8,128)(2,1)} %fusion.1) | data formatting | bytes 1638400 | tf_op jit(solution)/shard_map/convert_element_type | solution.py:49
  39.5 2.1 %copy.815 = bf16[128,25,128]{0,2,1:T(8,128)(2,1)S(1)} copy(bf16[128,25,128]{2,1,0:T(8,128)(2,1)} %fusion) | data formatting | bytes 1638400 | tf_op jit(solution)/shard_map/convert_element_type | solution.py:49
  46.7 38.1 %all-reduce.7.cloned.1.call-done = f32[8,16,128]{2,1,0:T(8,128)} async-done(((f32[8,16,128]{2,1,0:T(8,128)}), f32[8,16,128]{2,1,0:T(8,128)}) %all-reduce.7.cloned.1.call-update) | async-done | bytes 65552 | tf_op jit(solution)/shard_map/psum | solution.py:104
  85.8 1.3 collective-permute-start.2
  87.1 1.5 collective-permute-start.3
  89.7 2.2 %collective-permute-done.3 = bf16[2,16,128]{2,1,0:T(8,128)(2,1)S(1)} collective-permute-done((bf16[2,16,128]{2,1,0:T(8,128)(2,1)S(1)}, bf16[2,16,128]{2,1,0:T(8,128)(2,1)S(1)}, u32[]{:S(2)}, u32[]{:S(2)}) %collective-permute-start.3) | collective-permute-done | bytes 8224 | tf_op jit(solution)/shard_map/ppermute | solution.py:21
  91.9 2.0 %fusion.22 = f32[12,20,25,128]{3,1,2,0:T(8,128)S(1)} fusion(bf16[128,25,128]{0,1,2:T(8,128)(2,1)} %fusion.4, bf16[2,16,128]{2,1,0:T(8,128)(2,1)S(1)} %collective-permute-done.3, bf16[8,16,128]{2,1,0:T(8,128)(2,1)S(1)} %divide_convert_fusion.1, bf16[2,16,128]{2,1,0:T(8,128)(2,1)S(1)} %collective-permute-done.2), kind=kOutput, calls=%fused_computation.37 | convolution fusion | flops 196976640 | bytes 3940352 | tf_op jit(solution)/shard_map/dot_general | solution.py:50
  99.3 4.3 %collective-permute-start.4 = (bf16[4,2,16,128]{3,2,1,0:T(8,128)(2,1)S(1)}, bf16[4,2,16,128]{3,2,1,0:T(8,128)(2,1)S(1)}, u32[]{:S(2)}, u32[]{:S(2)}) collective-permute-start(bf16[4,2,16,128]{3,2,1,0:T(8,128)(2,1)S(1)} %get-tuple-element.17), channel_id=1, source_target_pairs={{0,1},{1,2},{2,3},{3,4},{4,5},{5,6},{6,7},{8,9},{9,10},{10,11},{11... | collective-permute-start | bytes 98312 | tf_op jit(solution)/shard_map/ppermute | solution.py:19
  103.6 1.3 collective-permute-start.5
  104.9 1.8 %collective-permute-done.5 = bf16[4,2,16,128]{3,2,1,0:T(8,128)(2,1)S(1)} collective-permute-done((bf16[4,2,16,128]{3,2,1,0:T(8,128)(2,1)S(1)}, bf16[4,2,16,128]{3,2,1,0:T(8,128)(2,1)S(1)}, u32[]{:S(2)}, u32[]{:S(2)}) %collective-permute-start.5) | collective-permute-done | bytes 32800 | tf_op jit(solution)/shard_map/ppermute | solution.py:21
  110.9 36.5 %all-reduce.9.cloned.1.call-done = f32[8,16,128]{2,1,0:T(8,128)} async-done(((f32[8,16,128]{2,1,0:T(8,128)}), f32[8,16,128]{2,1,0:T(8,128)}) %all-reduce.9.cloned.1.call-update) | async-done | bytes 65552 | tf_op jit(solution)/shard_map/psum | solution.py:104
  148.4 1.3 collective-permute-start.6
  149.6 1.3 collective-permute-start.7
  151.0 3.5 %collective-permute-done.7 = bf16[2,16,128]{2,1,0:T(8,128)(2,1)S(1)} collective-permute-done((bf16[2,16,128]{2,1,0:T(8,128)(2,1)S(1)}, bf16[2,16,128]{2,1,0:T(8,128)(2,1)S(1)}, u32[]{:S(2)}, u32[]{:S(2)}) %collective-permute-start.7) | collective-permute-done | bytes 8224 | tf_op jit(solution)/shard_map/ppermute | solution.py:21
  (105 shorter events, 34.5 us)
Async XLA Ops:
  6.5 78.3 %all-reduce.7.cloned.1.call-start = ((), (), s32[]{:S(2)}) async-start(), calls=%async_computation | async-start | bytes 131072 | tf_op jit(solution)/shard_map/psum | solution.py:104
  7.5 34.2 %collective-permute-start = (bf16[4,2,16,128]{3,2,1,0:T(8,128)(2,1)S(1)}, bf16[4,2,16,128]{3,2,1,0:T(8,128)(2,1)}, u32[]{:S(2)}, u32[]{:S(2)}) collective-permute-start(bf16[4,2,16,128]{3,2,1,0:T(8,128)(2,1)S(1)} %get-tuple-element.19), channel_id=1, source_target_pairs={{0,1},{1,2},{2,3},{3,4},{4,5},{5,6},{6,7},{8,9},{9,10},{10,11},{11... | collective-permute-start | bytes 98312 | tf_op jit(solution)/shard_map/ppermute | solution.py:19
  10.5 31.2 %collective-permute-start.1 = (bf16[4,2,16,128]{3,2,1,0:T(8,128)(2,1)S(1)}, bf16[4,2,16,128]{3,2,1,0:T(8,128)(2,1)}, u32[]{:S(2)}, u32[]{:S(2)}) collective-permute-start(bf16[4,2,16,128]{3,2,1,0:T(8,128)(2,1)S(1)} %get-tuple-element.20), channel_id=1, source_target_pairs={{1,0},{2,1},{3,2},{4,3},{5,4},{6,5},{7,6},{9,8},{10,9},{11,10},{12... | collective-permute-start | bytes 98312 | tf_op jit(solution)/shard_map/ppermute | solution.py:21
  46.6 47.2 %copy-start.7 = (f32[4,8,16,128]{3,2,1,0:T(8,128)S(1)}, f32[4,8,16,128]{3,2,1,0:T(8,128)}, u32[]{:S(2)}) copy-start(f32[4,8,16,128]{3,2,1,0:T(8,128)} %param.5) | copy-start | bytes 786436
  46.6 100.9 %all-reduce.9.cloned.1.call-start = ((), (), s32[]{:S(2)}) async-start(), calls=%async_computation.1 | async-start | bytes 131072 | tf_op jit(solution)/shard_map/psum | solution.py:104
  84.8 9.0 %copy-start.12 = (f32[8,16,128]{2,1,0:T(8,128)S(1)}, f32[8,16,128]{2,1,0:T(8,128)}, u32[]{:S(2)}) copy-start(f32[8,16,128]{2,1,0:T(8,128)} %fusion.281) | copy-start | bytes 196612
  84.8 9.9 %copy-start.5 = (bf16[128,25,128]{0,1,2:T(8,128)(2,1)S(1)}, bf16[128,25,128]{0,1,2:T(8,128)(2,1)}, u32[]{:S(2)}) copy-start(bf16[128,25,128]{0,1,2:T(8,128)(2,1)} %fusion.5) | copy-start | bytes 2457604
  85.8 3.9 %collective-permute-start.2 = (bf16[2,16,128]{2,1,0:T(8,128)(2,1)S(1)}, bf16[2,16,128]{2,1,0:T(8,128)(2,1)S(1)}, u32[]{:S(2)}, u32[]{:S(2)}) collective-permute-start(bf16[2,16,128]{2,1,0:T(8,128)(2,1)S(1)} %get-tuple-element.23), channel_id=1, source_target_pairs={{0,1},{1,2},{2,3},{3,4},{4,5},{5,6},{6,7},{8,9},{9,10},{10,11},{11... | collective-permute-start | bytes 24584 | tf_op jit(solution)/shard_map/ppermute | solution.py:19
  87.1 4.8 %collective-permute-start.3 = (bf16[2,16,128]{2,1,0:T(8,128)(2,1)S(1)}, bf16[2,16,128]{2,1,0:T(8,128)(2,1)S(1)}, u32[]{:S(2)}, u32[]{:S(2)}) collective-permute-start(bf16[2,16,128]{2,1,0:T(8,128)(2,1)S(1)} %get-tuple-element.24), channel_id=1, source_target_pairs={{1,0},{2,1},{3,2},{4,3},{5,4},{6,5},{7,6},{9,8},{10,9},{11,10},{12... | collective-permute-start | bytes 24584 | tf_op jit(solution)/shard_map/ppermute | solution.py:21
  89.6 8.9 %copy-start.14 = (f32[8,16,128]{2,1,0:T(8,128)}, f32[8,16,128]{2,1,0:T(8,128)S(1)}, u32[]{:S(2)}) copy-start(f32[8,16,128]{2,1,0:T(8,128)S(1)} %fusion.275) | copy-start | bytes 196612
  93.8 1.6 copy-start.10
  93.9 2.4 %copy-start.3 = (bf16[128,25,128]{0,1,2:T(8,128)(2,1)S(1)}, bf16[128,25,128]{0,1,2:T(8,128)(2,1)}, u32[]{:S(2)}) copy-start(bf16[128,25,128]{0,1,2:T(8,128)(2,1)} %fusion.6) | copy-start | bytes 2457604
  95.4 1.6 copy-start.8
  95.4 2.3 %copy-start.1 = (bf16[128,25,128]{0,1,2:T(8,128)(2,1)S(1)}, bf16[128,25,128]{0,1,2:T(8,128)(2,1)}, u32[]{:S(2)}) copy-start(bf16[128,25,128]{0,1,2:T(8,128)(2,1)} %fusion.7) | copy-start | bytes 2457604
  99.3 5.6 %collective-permute-start.4 = (bf16[4,2,16,128]{3,2,1,0:T(8,128)(2,1)S(1)}, bf16[4,2,16,128]{3,2,1,0:T(8,128)(2,1)S(1)}, u32[]{:S(2)}, u32[]{:S(2)}) collective-permute-start(bf16[4,2,16,128]{3,2,1,0:T(8,128)(2,1)S(1)} %get-tuple-element.17), channel_id=1, source_target_pairs={{0,1},{1,2},{2,3},{3,4},{4,5},{5,6},{6,7},{8,9},{9,10},{10,11},{11... | collective-permute-start | bytes 98312 | tf_op jit(solution)/shard_map/ppermute | solution.py:19
  103.6 3.1 %collective-permute-start.5 = (bf16[4,2,16,128]{3,2,1,0:T(8,128)(2,1)S(1)}, bf16[4,2,16,128]{3,2,1,0:T(8,128)(2,1)S(1)}, u32[]{:S(2)}, u32[]{:S(2)}) collective-permute-start(bf16[4,2,16,128]{3,2,1,0:T(8,128)(2,1)S(1)} %get-tuple-element.18), channel_id=1, source_target_pairs={{1,0},{2,1},{3,2},{4,3},{5,4},{6,5},{7,6},{9,8},{10,9},{11,10},{12... | collective-permute-start | bytes 98312 | tf_op jit(solution)/shard_map/ppermute | solution.py:21
  109.7 37.8 %copy-start.20 = (f32[8,16,128]{2,1,0:T(8,128)S(1)}, f32[8,16,128]{2,1,0:T(8,128)}, u32[]{:S(2)}) copy-start(f32[8,16,128]{2,1,0:T(8,128)} %param.6) | copy-start | bytes 196612
  109.7 44.8 %copy-start = (bf16[128,25,128]{0,1,2:T(8,128)(2,1)S(1)}, bf16[128,25,128]{0,1,2:T(8,128)(2,1)}, u32[]{:S(2)}) copy-start(bf16[128,25,128]{0,1,2:T(8,128)(2,1)} %fusion.4) | copy-start | bytes 2457604
  110.9 44.3 %copy-start.13 = (f32[8,16,128]{2,1,0:T(8,128)S(1)}, f32[8,16,128]{2,1,0:T(8,128)}, u32[]{:S(2)}) copy-start(f32[8,16,128]{2,1,0:T(8,128)} %fusion.281) | copy-start | bytes 196612
  110.9 44.3 %copy-start.19 = (f32[8,16,128]{2,1,0:T(8,128)S(1)}, f32[8,16,128]{2,1,0:T(8,128)}, u32[]{:S(2)}) copy-start(f32[8,16,128]{2,1,0:T(8,128)} %get-tuple-element.10) | copy-start | bytes 196612
  110.9 44.5 %copy-start.6 = (bf16[128,25,128]{0,1,2:T(8,128)(2,1)S(1)}, bf16[128,25,128]{0,1,2:T(8,128)(2,1)}, u32[]{:S(2)}) copy-start(bf16[128,25,128]{0,1,2:T(8,128)(2,1)} %fusion.5) | copy-start | bytes 2457604
  148.4 2.6 %collective-permute-start.6 = (bf16[2,16,128]{2,1,0:T(8,128)(2,1)S(1)}, bf16[2,16,128]{2,1,0:T(8,128)(2,1)S(1)}, u32[]{:S(2)}, u32[]{:S(2)}) collective-permute-start(bf16[2,16,128]{2,1,0:T(8,128)(2,1)S(1)} %get-tuple-element.21), channel_id=1, source_target_pairs={{0,1},{1,2},{2,3},{3,4},{4,5},{5,6},{6,7},{8,9},{9,10},{10,11},{11... | collective-permute-start | bytes 24584 | tf_op jit(solution)/shard_map/ppermute | solution.py:19
  149.6 4.8 %collective-permute-start.7 = (bf16[2,16,128]{2,1,0:T(8,128)(2,1)S(1)}, bf16[2,16,128]{2,1,0:T(8,128)(2,1)S(1)}, u32[]{:S(2)}, u32[]{:S(2)}) collective-permute-start(bf16[2,16,128]{2,1,0:T(8,128)(2,1)S(1)} %get-tuple-element.22), channel_id=1, source_target_pairs={{1,0},{2,1},{3,2},{4,3},{5,4},{6,5},{7,6},{9,8},{10,9},{11,10},{12... | collective-permute-start | bytes 24584 | tf_op jit(solution)/shard_map/ppermute | solution.py:21
  156.2 1.3 copy-start.2
  (7 other events, 7.5 us)
Sparse Core Ops, SparseCore 0:
  46.7 38.0 all-reduce.6
  111.0 36.3 all-reduce.8
where the time goes:
time: 169 us; the launch traced here: 166 us
  waiting for transfers between devices  82.2 us (49%)
  matrix products  27.4 us (16%)
  other arithmetic  18 us (11%)
  starting transfers between devices  15.2 us (9%)
  between operations  13.9 us (8%)
  local copies, waits for them, and re-layouts  9.22 us (5%)
    psum x2, waiting for transfers between devices, shards(): sensor = lax.psum(partial_sensor, 'depth')  74.7 us
    dot_general x16, matrix products, project(): jnp.dot(flat_plane, dense, preferred_element_type=jnp.float32)  12.6 us
    ppermute x4, starting transfers between devices, with_halo(): lax.ppermute(tail, axis, [(i, (i + 1) % count) for i in range(ends)])  9.85 us
    convert_element_type x4, local copies, waits for them, and re-layouts, project(): dense = dense.astype(jnp.bfloat16).reshape(pixels, span_all * pixels)  7.6 us
    ppermute x4, waiting for transfers between devices, with_halo(): lax.ppermute(head, axis, [((i + 1) % count, i) for i in range(ends)])  7.46 us
    dot_general x4, matrix products, project(): jnp.einsum('ko,kji->ioj', one_hot, block_values, precision=lax.Precision....  6.06 us
    ppermute x4, starting transfers between devices, with_halo(): lax.ppermute(head, axis, [((i + 1) % count, i) for i in range(ends)])  5.34 us
    dot_general x4, matrix products, project(): jnp.einsum('ko,kji->joi', one_hot, block_values, precision=lax.Precision....  5.09 us
  transfers between devices with their start and end apart: 10, of which 5 were waited for; matrix products, arithmetic and copies ran while one was open for 19% of the time, Pallas kernels for 0%

commit v1 on v0

v1 whole, which is shorter than its diff:
```python
import functools

import jax
import jax.numpy as jnp
from jax import lax
from jax.experimental import pallas as pl
from jax.experimental.pallas import tpu as pltpu
from jax.sharding import PartitionSpec as P

RY = 2
RX = 2
SX = 2 * RX + 1
ITERS = 2
MESH = pl.DeviceIdType.MESH


def kernel(
    D, L, planes, slots, rows, cols,
    at_ref, vol_hbm, meas_hbm, psf_hbm, out_ref,
    w, vol, meas, cov, xs, rs, cs, part, recv_own, recv_halo, rchunk, rext, total,
    load_sem, s_own, r_own, s_halo, r_halo, s_rat, s_rath, r_rat,
):
    d = lax.axis_index("depth")
    b = lax.axis_index("lat")
    pix = 128
    own = rows * cols
    chunk = own // D
    halo = RY * cols
    h = halo // chunk
    ext = own + 2 * halo
    out_rows = rows + 2 * RY
    f_zero = rows + 2 * RY
    f_rows = f_zero + out_rows
    b_rows = rows + 2 * RY + rows
    b_zero = rows + 2 * RY
    up = lax.rem(b + L - 1, L)
    down = lax.rem(b + 1, L)
    has_up = b > 0
    has_down = b < L - 1
    first = d < h
    last = d >= D - h

    loads = [pltpu.make_async_copy(vol_hbm, vol, load_sem.at[planes])]
    for p in range(planes):
        loads.append(
            pltpu.make_async_copy(
                psf_hbm.at[p], w.at[pl.ds(p * slots, slots)], load_sem.at[p]
            )
        )
    loads.append(
        pltpu.make_async_copy(
            meas_hbm.at[pl.ds(pl.multiple_of(d * chunk, chunk), chunk)],
            meas,
            load_sem.at[planes + 1],
        )
    )
    for copy in loads:
        copy.start()

    barrier = pltpu.get_barrier_semaphore()

    def greet(to_d, to_b):
        pl.semaphore_signal(barrier, inc=1, device_id=(to_d, to_b), device_id_type=MESH)

    for t in range(1, D):
        greet(lax.rem(d + t, D), b)

    @pl.when(has_up)
    def _():
        for c in range(D - h, D):
            greet(c, up)

    @pl.when(has_up & first)
    def _():
        for c in range(D - h):
            greet(c, up)

    @pl.when(has_down)
    def _():
        for c in range(h):
            greet(c, down)

    @pl.when(has_down & last)
    def _():
        for c in range(h, D):
            greet(c, down)

    fwd_at = [at_ref[0, d * planes + p, k] for p in range(planes) for k in range(slots)]
    back_at = [at_ref[1, d * planes + p, k] for p in range(planes) for k in range(slots)]

    def zeros(count):
        return jnp.zeros((count, cols, pix), jnp.bfloat16)

    for p in range(planes):
        for s in range(SX):
            xs[p, pl.ds(s * f_rows, 2 * RY)] = zeros(2 * RY)
            xs[p, pl.ds(s * f_rows + 2 * RY + rows, f_rows - 2 * RY - rows)] = zeros(
                f_rows - 2 * RY - rows
            )
    for s in range(SX):
        rs[pl.ds(s * b_rows + b_zero, rows)] = zeros(rows)
        cs[pl.ds(s * b_rows + b_zero, rows)] = zeros(rows)

    def shifted(flat, s):
        count = flat.shape[0]
        move = s - RX
        if move:
            col = lax.broadcasted_iota(jnp.int32, (count, pix), 0) % cols + move
            flat = pltpu.roll(flat, (-move) % count, 0)
            flat = jnp.where((col >= 0) & (col < cols), flat, 0.0)
        return flat.astype(jnp.bfloat16).reshape(count // cols, cols, pix)

    def spread_plane(p, plane):
        for s in range(SX):
            xs[p, pl.ds(s * f_rows + 2 * RY, rows)] = shifted(plane, s)

    def spread_ratio(ref, flat):
        for s in range(SX):
            ref[pl.ds(s * b_rows, out_rows)] = shifted(flat, s)

    def forward():
        acc = jnp.zeros((ext, pix), jnp.float32)
        q = 0
        while q < planes * slots:
            step = min(2, planes * slots - q)
            wins = [
                xs[i // slots, pl.ds(fwd_at[i], out_rows)].reshape(ext, pix)
                for i in range(q, q + step)
            ]
            lhs = jnp.concatenate(wins, axis=1) if step > 1 else wins[0]
            rhs = w[pl.ds(q, step)].reshape(step * pix, pix)
            acc = acc + jnp.dot(lhs, rhs, preferred_element_type=jnp.float32)
            q += step
        return acc

    def backward(ref, p):
        acc = jnp.zeros((own, pix), jnp.float32)
        k = 0
        while k < slots:
            step = min(2, slots - k)
            ids = [p * slots + i for i in range(k, k + step)]
            wins = [ref[pl.ds(back_at[i], rows)].reshape(own, pix) for i in ids]
            mats = [w[i] for i in ids]
            lhs = jnp.concatenate(wins, axis=1) if step > 1 else wins[0]
            rhs = jnp.concatenate(mats, axis=1) if step > 1 else mats[0]
            acc = acc + lax.dot_general(
                lhs, rhs, (((1,), (1,)), ((), ())), preferred_element_type=jnp.float32
            )
            k += step
        return acc

    def remote(src, dst, send, recv, to_d, to_b):
        return pltpu.make_async_remote_copy(
            src_ref=src,
            dst_ref=dst,
            send_sem=send,
            recv_sem=recv,
            device_id=(to_d, to_b),
            device_id_type=MESH,
        )

    def own_copy(it, t):
        c = lax.rem(d + t, D)
        return remote(
            part.at[it, h + c], recv_own.at[it, d], s_own.at[it, t], r_own.at[it, d], c, b
        )

    def own_arrival(it, t):
        c = lax.rem(d + t, D)
        return remote(
            part.at[it, h + c], recv_own.at[it, c], s_own.at[it, t], r_own.at[it, c], c, b
        )

    def up_copy(it, t):
        return remote(
            part.at[it, t], recv_halo.at[it, d], s_halo.at[it, t], r_halo.at[it, d],
            D - h + t, up,
        )

    def down_copy(it, t):
        return remote(
            part.at[it, h + D + t], recv_halo.at[it, d], s_halo.at[it, h + t],
            r_halo.at[it, d], t, down,
        )

    def halo_arrival(it, c, to_b):
        return remote(
            part.at[it, 0], recv_halo.at[it, c], s_halo.at[it, 0], r_halo.at[it, c], c, to_b
        )

    def ratio_copy(it, t):
        c = lax.rem(d + t, D)
        return remote(
            rchunk.at[it], rext.at[it, h + d], s_rat.at[it, t], r_rat.at[it, h + d], c, b
        )

    def ratio_arrival(it, slot, to_d, to_b):
        return remote(
            rchunk.at[it], rext.at[it, slot], s_rat.at[it, 0], r_rat.at[it, slot], to_d, to_b
        )

    def ratio_up(it, c):
        slot = h + D + lax.rem(d, h)
        return remote(
            rchunk.at[it], rext.at[it, slot], s_rath.at[it, c], r_rat.at[it, slot], c, up
        )

    def ratio_down(it, c):
        slot = lax.rem(d + h, D)
        return remote(
            rchunk.at[it], rext.at[it, slot], s_rath.at[it, c], r_rat.at[it, slot], c, down
        )

    ext_row = lax.broadcasted_iota(jnp.int32, (ext, pix), 0)
    low = jnp.where(has_up, 0, halo)
    high = jnp.where(has_down, ext, halo + own)
    spread_ratio(cs, jnp.where((ext_row >= low) & (ext_row < high), 1.0, 0.0))

    loads[0].wait()
    for p in range(planes):
        spread_plane(p, vol[p])

    for copy in loads[1:]:
        copy.wait()

    for it in range(ITERS):
        part[it] = forward().reshape(D + 2 * h, chunk, pix)
        if it == 0:
            amount = (
                (D - 1)
                + jnp.where(has_up, jnp.where(first, D, h), 0)
                + jnp.where(has_down, jnp.where(last, D, h), 0)
            )
            pl.semaphore_wait(barrier, amount)

        @pl.when(has_up)
        def _():
            for t in range(h):
                up_copy(it, t).start()

        @pl.when(has_down)
        def _():
            for t in range(h):
                down_copy(it, t).start()

        for t in range(1, D):
            own_copy(it, t).start()

        if it == 0:
            for p in range(planes):
                cov[p] = backward(cs, p)

        sensor = part[it, h + d]
        for t in range(1, D):
            own_arrival(it, t).wait_recv()
            sensor = sensor + recv_own[it, lax.rem(d + t, D)]

        @pl.when(has_up & first)
        def _():
            for c in range(D):
                halo_arrival(it, c, up).wait_recv()

        @pl.when(has_down & last)
        def _():
            for c in range(D):
                halo_arrival(it, c, down).wait_recv()

        total[...] = sensor

        @pl.when((has_up & first) | (has_down & last))
        def _():
            more = recv_halo[it, 0]
            for c in range(1, D):
                more = more + recv_halo[it, c]
            total[...] += more

        ratio = (meas[...] / total[...]).astype(jnp.bfloat16)
        rchunk[it] = ratio
        rext[it, h + d] = ratio

        @pl.when(has_up & first)
        def _():
            for c in range(D):
                ratio_up(it, c).start()

        @pl.when(has_down & last)
        def _():
            for c in range(D):
                ratio_down(it, c).start()

        for t in range(1, D):
            ratio_copy(it, t).start()

        @pl.when(has_up)
        def _():
            for t in range(h):
                ratio_arrival(it, t, D - h + t, up).wait_recv()

        @pl.when(jnp.logical_not(has_up))
        def _():
            for t in range(h):
                rext[it, t] = jnp.zeros((chunk, pix), jnp.bfloat16)

        @pl.when(has_down)
        def _():
            for t in range(h):
                ratio_arrival(it, h + D + t, t, down).wait_recv()

        @pl.when(jnp.logical_not(has_down))
        def _():
            for t in range(h):
                rext[it, h + D + t] = jnp.zeros((chunk, pix), jnp.bfloat16)

        for t in range(1, D):
            c = lax.rem(d + t, D)
            ratio_arrival(it, h + c, c, b).wait_recv()

        spread_ratio(rs, rext[it].astype(jnp.float32).reshape(ext, pix))
        for p in range(planes):
            plane = vol[p] * backward(rs, p) / cov[p]
            if it < ITERS - 1:
                vol[p] = plane
                spread_plane(p, plane)
            else:
                out_ref[p] = plane

    for it in range(ITERS):
        for t in range(1, D):
            own_copy(it, t).wait_send()
            ratio_copy(it, t).wait_send()

        @pl.when(has_up)
        def _():
            for t in range(h):
                up_copy(it, t).wait_send()

        @pl.when(has_down)
        def _():
            for t in range(h):
                down_copy(it, t).wait_send()

        @pl.when(has_up & first)
        def _():
            for c in range(D):
                ratio_up(it, c).wait_send()

        @pl.when(has_down & last)
        def _():
            for c in range(D):
                ratio_down(it, c).wait_send()


def shards(D, L, volume_init, measured, psf, offsets, counts):
    planes, rows, cols, pix = volume_init.shape
    slots = psf.shape[1]
    own = rows * cols
    chunk = own // D
    h = RY * cols // chunk
    f_rows = 2 * (rows + 2 * RY)
    b_rows = 2 * rows + 2 * RY
    row = offsets // SX
    col = offsets % SX
    alive = jnp.arange(slots, dtype=jnp.int32)[None, :] < counts[:, None]
    zero_at = rows + 2 * RY
    table = jnp.stack(
        [
            jnp.where(alive, col * f_rows + row, zero_at),
            jnp.where(alive, (SX - 1 - col) * b_rows + (2 * RY - row), zero_at),
        ]
    )
    dma = pltpu.SemaphoreType.DMA
    out = pl.pallas_call(
        functools.partial(kernel, D, L, planes, slots, rows, cols),
        out_shape=jax.ShapeDtypeStruct((planes, own, pix), jnp.float32),
        in_specs=[pl.BlockSpec(memory_space=pltpu.SMEM)]
        + [pl.BlockSpec(memory_space=pl.ANY)] * 3,
        out_specs=pl.BlockSpec(memory_space=pltpu.VMEM),
        scratch_shapes=[
            pltpu.VMEM((planes * slots, pix, pix), jnp.bfloat16),
            pltpu.VMEM((planes, own, pix), jnp.float32),
            pltpu.VMEM((chunk, pix), jnp.float32),
            pltpu.VMEM((planes, own, pix), jnp.float32),
            pltpu.VMEM((planes, SX * f_rows, cols, pix), jnp.bfloat16),
            pltpu.VMEM((SX * b_rows, cols, pix), jnp.bfloat16),
            pltpu.VMEM((SX * b_rows, cols, pix), jnp.bfloat16),
            pltpu.VMEM((ITERS, D + 2 * h, chunk, pix), jnp.float32),
            pltpu.VMEM((ITERS, D, chunk, pix), jnp.float32),
            pltpu.VMEM((ITERS, D, chunk, pix), jnp.float32),
            pltpu.VMEM((ITERS, chunk, pix), jnp.bfloat16),
            pltpu.VMEM((ITERS, D + 2 * h, chunk, pix), jnp.bfloat16),
            pltpu.VMEM((chunk, pix), jnp.float32),
            dma((planes + 2,)),
            dma((ITERS, D)),
            dma((ITERS, D)),
            dma((ITERS, 2 * h)),
            dma((ITERS, D)),
            dma((ITERS, D)),
            dma((ITERS, D)),
            dma((ITERS, D + 2 * h)),
        ],
        compiler_params=pltpu.CompilerParams(
            collective_id=0, has_side_effects=True, vmem_limit_bytes=32 * 1024 * 1024
        ),
    )(
        table,
        volume_init.reshape(planes, own, pix),
        measured.reshape(own, pix),
        psf,
    )
    return out.reshape(planes, rows, cols, pix)


def solution(mesh):
    return jax.shard_map(
        functools.partial(shards, mesh.shape["depth"], mesh.shape["lat"]),
        mesh=mesh,
        in_specs=(
            P("depth", "lat", None, None),
            P("lat", None, None),
            P("depth", None, None, None),
            P(),
            P(),
        ),
        out_specs=P("depth", "lat", None, None),
        check_vma=False,
    )
```

time: 169 us -> 31 us (0.18); the launches traced: 166 us -> 30.7 us
  waiting for transfers between devices: 82.2 us -> 0 us
  matrix products: 27.4 us -> 0 us
  Pallas kernels: 0 us -> 26 us
  other arithmetic: 18 us -> 0.78 us
  starting transfers between devices: 15.2 us -> 0 us
  between operations: 13.9 us -> 0.02 us
  local copies, waits for them, and re-layouts: 9.22 us -> 3.94 us
    psum x2 -> x0, waiting for transfers between devices: 74.7 us -> none  [shards(): sensor = lax.psum(partial_sensor, 'depth')]
    dot_general x28 -> x0, matrix products: 27.4 us -> none  [the longest x16 12.6 us: project(): jnp.dot(flat_plane, dense, preferred_element_type=jnp.float32)]
    pallas_call x0 -> x1, Pallas kernels: none -> 26 us  [shards(): pl.pallas_call(functools.partial(kernel, D, L, planes, slots, rows, cols)...]
    ppermute x8 -> x0, starting transfers between devices: 15.2 us -> none  [the longest x4 9.85 us: with_halo(): lax.ppermute(tail, axis, [(i, (i + 1) % count) for i in range(ends)])]
    convert_element_type x4 -> x0, local copies, waits for them, and re-layouts: 7.6 us -> none  [project(): dense = dense.astype(jnp.bfloat16).reshape(pixels, span_all * pixels)]
    ppermute x8 -> x0, waiting for transfers between devices: 7.47 us -> none  [the longest x4 7.46 us: with_halo(): lax.ppermute(head, axis, [((i + 1) % count, i) for i in range(ends)])]
    another operation x9 -> x2, other arithmetic: 4.54 us -> 0.78 us  [shards(): jnp.stack([jnp.where(alive, col * f_rows + row, zero_at), jnp.where(alive...]
    unnamed x42 -> x7, local copies, waits for them, and re-layouts: 0.27 us -> 3.94 us
  transfers between devices with their start and end apart: 10 -> 0, of which waited for: 5 -> 0; matrix products, arithmetic and copies ran while one was open for 19% -> 0% of each run, Pallas kernels for 0% -> 0%
where the time goes in v1:
time: 31 us; the launch traced here: 30.7 us
  Pallas kernels  26 us (84%)
  local copies, waits for them, and re-layouts  3.94 us (13%)
  other arithmetic  0.78 us (3%)
    pallas_call x1, Pallas kernels, shards(): pl.pallas_call(functools.partial(kernel, D, L, planes, slots, rows, cols)...  26 us
    unnamed x7, local copies, waits for them, and re-layouts  3.94 us
    another operation x2, other arithmetic, shards(): jnp.stack([jnp.where(alive, col * f_rows + row, zero_at), jnp.where(alive...  0.78 us

profile of v1, /device:TPU:0, one launch (start us, length us, event | category | flops | bytes accessed | tf_op | source)
XLA Modules:
  0.0 30.7 jit_solution(4146199035396138716)
XLA Ops:
  0.0 0.8 %select_bitcast_fusion.1 = (s32[1,16,13]{2,1,0:T(8,128)S(1)}, s32[1,16,13]{2,1,0:T(8,128)S(1)}) fusion(s32[16,13]{1,0:T(8,128)} %param.8, s32[16]{0:T(128)} %param.9), kind=kLoop, calls=%fused_computation.4 | loop fusion | flops 4368 | bytes 2560 | tf_op jit(solution)/shard_map/stack | solution.py:365
  0.8 0.0 copy-start
  0.8 1.4 %copy-done = bf16[4,13,128,128]{3,2,1,0:T(8,128)(2,1)S(1)} copy-done((bf16[4,13,128,128]{3,2,1,0:T(8,128)(2,1)S(1)}, bf16[4,13,128,128]{3,2,1,0:T(8,128)(2,1)}, u32[]{:S(2)}) %copy-start) | copy-done | bytes 1703960
  2.2 0.0 copy-start.1
  2.2 0.9 %copy-done.1 = f32[4,8,16,128]{3,2,1,0:T(8,128)S(1)} copy-done((f32[4,8,16,128]{3,2,1,0:T(8,128)S(1)}, f32[4,8,16,128]{3,2,1,0:T(8,128)}, u32[]{:S(2)}) %copy-start.1) | copy-done | bytes 262168
  3.2 0.0 copy-start.2
  3.2 0.8 %copy-done.2 = f32[8,16,128]{2,1,0:T(8,128)S(1)} copy-done((f32[8,16,128]{2,1,0:T(8,128)S(1)}, f32[8,16,128]{2,1,0:T(8,128)}, u32[]{:S(2)}) %copy-start.2) | copy-done | bytes 65560
  4.0 26.0 %shard_map.55 = f32[4,128,128]{2,1,0:T(8,128)S(1)} custom-call(s32[2,16,13]{2,1,0:T(8,128)S(1)} %pad_add_fusion.at_ref, f32[4,128,128]{2,1,0:T(8,128)S(1)} %bitcast.8, f32[128,128]{1,0:T(8,128)S(1)} %bitcast.9, bf16[4,13,128,128]{3,2,1,0:T(8,128)(2,1)S(1)} %copy-done), custom_call_target="tpu_custom_call" | custom-call | tf_op jit(solution)/shard_map/pallas_call | solution.py:372
  30.0 0.7 %copy.7 = f32[4,8,16,128]{3,2,1,0:T(8,128)} copy(f32[4,8,16,128]{3,2,1,0:T(8,128)S(1)} %bitcast.7) | data formatting | bytes 524288
  (1 shorter events, 0.0 us)
Async XLA Ops:
  0.8 1.5 %copy-start = (bf16[4,13,128,128]{3,2,1,0:T(8,128)(2,1)S(1)}, bf16[4,13,128,128]{3,2,1,0:T(8,128)(2,1)}, u32[]{:S(2)}) copy-start(bf16[4,13,128,128]{3,2,1,0:T(8,128)(2,1)} %psf_hbm.1) | copy-start | bytes 5111812
  2.2 0.9 %copy-start.1 = (f32[4,8,16,128]{3,2,1,0:T(8,128)S(1)}, f32[4,8,16,128]{3,2,1,0:T(8,128)}, u32[]{:S(2)}) copy-start(f32[4,8,16,128]{3,2,1,0:T(8,128)} %param.5) | copy-start | bytes 786436
  3.2 0.8 %copy-start.2 = (f32[8,16,128]{2,1,0:T(8,128)S(1)}, f32[8,16,128]{2,1,0:T(8,128)}, u32[]{:S(2)}) copy-start(f32[8,16,128]{2,1,0:T(8,128)} %param.6) | copy-start | bytes 196612

commit v2 on v1

--- a/solution.py
+++ b/solution.py
@@ -223,6 +223,8 @@
     for copy in loads[1:]:
         copy.wait()
 
+    early = planes // 2
+
     for it in range(ITERS):
         part[it] = forward().reshape(D + 2 * h, chunk, pix)
         if it == 0:
@@ -247,7 +249,7 @@
             own_copy(it, t).start()
 
         if it == 0:
-            for p in range(planes):
+            for p in range(early):
                 cov[p] = backward(cs, p)
 
         sensor = part[it, h + d]
@@ -290,6 +292,10 @@
 
         for t in range(1, D):
             ratio_copy(it, t).start()
+
+        if it == 0:
+            for p in range(early, planes):
+                cov[p] = backward(cs, p)
 
         @pl.when(has_up)
         def _():
@@ -368,12 +374,13 @@
             jnp.where(alive, (SX - 1 - col) * b_rows + (2 * RY - row), zero_at),
         ]
     )
+    in_hbm = functools.partial(pltpu.with_memory_space_constraint, memory_space=pltpu.HBM)
     dma = pltpu.SemaphoreType.DMA
     out = pl.pallas_call(
         functools.partial(kernel, D, L, planes, slots, rows, cols),
         out_shape=jax.ShapeDtypeStruct((planes, own, pix), jnp.float32),
         in_specs=[pl.BlockSpec(memory_space=pltpu.SMEM)]
-        + [pl.BlockSpec(memory_space=pl.ANY)] * 3,
+        + [pl.BlockSpec(memory_space=pltpu.HBM)] * 3,
         out_specs=pl.BlockSpec(memory_space=pltpu.VMEM),
         scratch_shapes=[
             pltpu.VMEM((planes * slots, pix, pix), jnp.bfloat16),
@@ -403,9 +410,9 @@
         ),
     )(
         table,
-        volume_init.reshape(planes, own, pix),
-        measured.reshape(own, pix),
-        psf,
+        in_hbm(volume_init.reshape(planes, own, pix)),
+        in_hbm(measured.reshape(own, pix)),
+        in_hbm(psf),
     )
     return out.reshape(planes, rows, cols, pix)
 

time: 31 us -> 26.7 us (0.86)
  local copies, waits for them, and re-layouts: 3.94 us -> 0.71 us
  Pallas kernels: 26 us -> 25 us
    unnamed x7 -> x1, local copies, waits for them, and re-layouts: 3.94 us -> 0.71 us
    pallas_call x1, Pallas kernels: 26 us -> 25 us  [shards(): pl.pallas_call(functools.partial(kernel, D, L, planes, slots, rows, cols)...]
where the time goes in v2:
time: 26.7 us; the launch traced here: 26.5 us
  Pallas kernels  25 us (94%)
  other arithmetic  0.78 us (3%)
  local copies, waits for them, and re-layouts  0.71 us (3%)
    pallas_call x1, Pallas kernels, shards(): pl.pallas_call(functools.partial(kernel, D, L, planes, slots, rows, cols)...  25 us
    another operation x2, other arithmetic, shards(): jnp.stack([jnp.where(alive, col * f_rows + row, zero_at), jnp.where(alive...  0.78 us
    unnamed x1, local copies, waits for them, and re-layouts  0.71 us

profile of v2, /device:TPU:0, one launch (start us, length us, event | category | flops | bytes accessed | tf_op | source)
XLA Modules:
  0.0 26.5 jit_solution(10457390121389483113)
XLA Ops:
  0.0 0.8 %select_bitcast_fusion.1 = (s32[1,16,13]{2,1,0:T(8,128)S(1)}, s32[1,16,13]{2,1,0:T(8,128)S(1)}) fusion(s32[16,13]{1,0:T(8,128)} %param.8, s32[16]{0:T(128)} %param.9), kind=kLoop, calls=%fused_computation.4 | loop fusion | flops 4368 | bytes 2560 | tf_op jit(solution)/shard_map/stack | solution.py:371
  0.8 25.0 %shard_map.55 = f32[4,128,128]{2,1,0:T(8,128)S(1)} custom-call(s32[2,16,13]{2,1,0:T(8,128)S(1)} %pad_add_fusion.at_ref, f32[4,128,128]{2,1,0:T(8,128)} %bitcast.8, f32[128,128]{1,0:T(8,128)} %bitcast.9, bf16[4,13,128,128]{3,2,1,0:T(8,128)(2,1)} %psf_hbm.1), custom_call_target="tpu_custom_call" | custom-call | tf_op jit(solution)/shard_map/pallas_call | solution.py:379
  25.8 0.7 %copy.7 = f32[4,8,16,128]{3,2,1,0:T(8,128)} copy(f32[4,8,16,128]{3,2,1,0:T(8,128)S(1)} %bitcast.7) | data formatting | bytes 524288
  (1 shorter events, 0.0 us)

commit v3 on v2

--- a/solution.py
+++ b/solution.py
@@ -118,11 +118,15 @@
         for s in range(SX):
             ref[pl.ds(s * b_rows, out_rows)] = shifted(flat, s)
 
-    def forward():
+    def forward(arriving):
+        landed = 0
         acc = jnp.zeros((ext, pix), jnp.float32)
         q = 0
         while q < planes * slots:
-            step = min(2, planes * slots - q)
+            step = min(4, planes * slots - q)
+            while arriving and landed * slots < q + step:
+                landed += 1
+                loads[landed].wait()
             wins = [
                 xs[i // slots, pl.ds(fwd_at[i], out_rows)].reshape(ext, pix)
                 for i in range(q, q + step)
@@ -137,7 +141,7 @@
         acc = jnp.zeros((own, pix), jnp.float32)
         k = 0
         while k < slots:
-            step = min(2, slots - k)
+            step = min(4, slots - k)
             ids = [p * slots + i for i in range(k, k + step)]
             wins = [ref[pl.ds(back_at[i], rows)].reshape(own, pix) for i in ids]
             mats = [w[i] for i in ids]
@@ -220,14 +224,12 @@
     for p in range(planes):
         spread_plane(p, vol[p])
 
-    for copy in loads[1:]:
-        copy.wait()
-
     early = planes // 2
 
     for it in range(ITERS):
-        part[it] = forward().reshape(D + 2 * h, chunk, pix)
+        part[it] = forward(it == 0).reshape(D + 2 * h, chunk, pix)
         if it == 0:
+            loads[planes + 1].wait()
             amount = (
                 (D - 1)
                 + jnp.where(has_up, jnp.where(first, D, h), 0)

time: 26.7 us -> 26.7 us (level)
  no operation moved by 1% of the time
where the time goes in v3:
time: 26.7 us; the launch traced here: 26.5 us
  Pallas kernels  25 us (94%)
  other arithmetic  0.78 us (3%)
  local copies, waits for them, and re-layouts  0.71 us (3%)
    pallas_call x1, Pallas kernels, shards(): pl.pallas_call(functools.partial(kernel, D, L, planes, slots, rows, cols)...  25 us
    another operation x2, other arithmetic, shards(): jnp.stack([jnp.where(alive, col * f_rows + row, zero_at), jnp.where(alive...  0.78 us
    unnamed x1, local copies, waits for them, and re-layouts  0.71 us

profile of v3, /device:TPU:0, one launch (start us, length us, event | category | flops | bytes accessed | tf_op | source)
XLA Modules:
  0.0 26.5 jit_solution(8286328987286675669)
XLA Ops:
  0.0 0.8 %select_bitcast_fusion.1 = (s32[1,16,13]{2,1,0:T(8,128)S(1)}, s32[1,16,13]{2,1,0:T(8,128)S(1)}) fusion(s32[16,13]{1,0:T(8,128)} %param.8, s32[16]{0:T(128)} %param.9), kind=kLoop, calls=%fused_computation.4 | loop fusion | flops 4368 | bytes 2560 | tf_op jit(solution)/shard_map/stack | solution.py:373
  0.8 25.0 %shard_map.55 = f32[4,128,128]{2,1,0:T(8,128)S(1)} custom-call(s32[2,16,13]{2,1,0:T(8,128)S(1)} %pad_add_fusion.at_ref, f32[4,128,128]{2,1,0:T(8,128)} %bitcast.8, f32[128,128]{1,0:T(8,128)} %bitcast.9, bf16[4,13,128,128]{3,2,1,0:T(8,128)(2,1)} %psf_hbm.1), custom_call_target="tpu_custom_call" | custom-call | tf_op jit(solution)/shard_map/pallas_call | solution.py:381
  25.8 0.7 %copy.7 = f32[4,8,16,128]{3,2,1,0:T(8,128)} copy(f32[4,8,16,128]{3,2,1,0:T(8,128)S(1)} %bitcast.7) | data formatting | bytes 524288
  (1 shorter events, 0.0 us)
